TPU v7x, 32 devices: a whole 2x2x4 slice. The times are simulated.
32 devices in a mesh: replica: 4 (over y, core), shard: 8 (over z, x).
Axes of the slice: x: 2, y: 2, z: 4, core: 2. Of those that a mesh axis runs over, the one named last changes fastest.
Arguments:
- tokens: bfloat16 [4, 1024, 3072], P('replica', 'shard'), may hold values from -6 to 6
- weight_slots: bfloat16 [4, 576, 128, 128], P('replica', 'shard'), may hold values from -0.15625 to 0.15625
- block_rows: int32 [96, 12], replicated, may hold values from 0 to 23, as said below
- block_owner: int32 [96, 12], replicated, may hold values from 0 to 7, as said below
- block_slot: int32 [96, 12], replicated, may hold values from 0 to 71, as said below
- grad_act: bfloat16 [4, 1024, 12288], P(None, 'shard', 'replica'), may hold values from -6 to 6
Outputs:
- act_out: bfloat16 [4, 1024, 12288], P(None, 'shard', 'replica')
- grad_tokens: bfloat16 [4, 1024, 3072], P('replica', 'shard')
- grad_slots: float32 [4, 576, 128, 128], P('replica', 'shard')
Inputs may be any that keep to these rules, and one draw needn't show every extreme that they name: `block_rows`: each row holds 12 distinct increasing block rows; within each group of 24 consecutive block columns every block row appears in exactly 12 of them. `block_owner`: within each group of 24 consecutive block columns no owner holds more than 72 blocks, and in every group some owner holds exactly 72. `block_slot`: within each group of 24 consecutive block columns the pairs of owner and slot are distinct.
All inputs are finite; a program needn't handle non-finite values.
Results may differ from a plain program's by a relative error of at most 0.01.
Values may be sent and summed in bfloat16 or wider, within the bound.
A program may use at most 192 MiB of HBM per device.

v0:
```python
import math
import jax
import jax.numpy as jnp
from jax import lax
from jax.sharding import PartitionSpec as P


def gelu_value(hidden):
    return 0.5 * hidden * (1.0 + lax.erf(hidden * 0.7071067811865476))


def gelu_slope(hidden):
    normal_cdf = 0.5 * (1.0 + lax.erf(hidden * 0.7071067811865476))
    return normal_cdf + hidden * jnp.exp(-0.5 * hidden * hidden) * 0.3989422804014327


def local(tokens, weight_slots, block_rows, block_owner, block_slot, grad_act):
    replica_count = lax.axis_size("replica")
    shard_count = lax.axis_size("shard")
    replica_index = lax.axis_index("replica")
    block_size = weight_slots.shape[3]
    capacity = weight_slots.shape[1]
    tok_rows = tokens.shape[1]
    model_width = tokens.shape[2]
    row_blocks = model_width // block_size
    keep_count = block_rows.shape[1]
    slice_cols = grad_act.shape[2] // block_size
    all_rows = replica_count * tok_rows
    own_slots = weight_slots.reshape(capacity, block_size, block_size)
    start_col = replica_index * slice_cols
    rows_here = lax.dynamic_slice_in_dim(block_rows, start_col, slice_cols, 0)
    owner_here = lax.dynamic_slice_in_dim(block_owner, start_col, slice_cols, 0)
    slot_here = lax.dynamic_slice_in_dim(block_slot, start_col, slice_cols, 0)
    place_here = owner_here * capacity + slot_here
    owner_slab = lax.all_gather(own_slots, "shard", axis=0, tiled=True)
    weight_cols = jnp.take(owner_slab, place_here.reshape(-1), axis=0)
    weight_cols = weight_cols.reshape(slice_cols, keep_count * block_size, block_size)
    gathered = lax.all_gather(tokens, "replica", axis=0, tiled=True)
    token_blocks = gathered.reshape(all_rows, row_blocks, block_size)
    cot_cols = jnp.transpose(grad_act.reshape(all_rows, slice_cols, block_size), (1, 0, 2))

    def column_step(grad_rows, inputs):
        rows_col, weight_col, cot_col = inputs
        col_inputs = jnp.take(token_blocks, rows_col, axis=1).reshape(
            all_rows, keep_count * block_size
        )
        hidden = jnp.dot(col_inputs, weight_col, preferred_element_type=jnp.float32)
        act_col = gelu_value(hidden).astype(jnp.bfloat16)
        slope = (cot_col.astype(jnp.float32) * gelu_slope(hidden)).astype(jnp.bfloat16)
        block_grad = lax.dot_general(
            col_inputs, slope, (((0,), (0,)), ((), ())), preferred_element_type=jnp.float32
        )
        back = lax.dot_general(
            slope, weight_col, (((1,), (1,)), ((), ())), preferred_element_type=jnp.float32
        )
        grad_rows = grad_rows.at[:, rows_col].add(back.reshape(all_rows, keep_count, block_size))
        return (grad_rows, (act_col, block_grad))

    start_rows = jnp.zeros((all_rows, row_blocks, block_size), jnp.float32)
    grad_rows, (act_cols, grad_blocks) = lax.scan(
        column_step, start_rows, (rows_here, weight_cols, cot_cols)
    )
    partial_grad = grad_rows.reshape(replica_count, tok_rows, model_width)
    grad_tokens = lax.psum_scatter(
        partial_grad.astype(jnp.bfloat16), "replica", scatter_dimension=0, tiled=True
    )
    grad_scale = 1.0 / math.sqrt(replica_count * shard_count * tok_rows)
    total_blocks = slice_cols * keep_count
    grad_flat = grad_blocks.reshape(total_blocks, block_size, block_size)
    slot_grid = jnp.zeros((shard_count * capacity, block_size, block_size), jnp.float32)
    slot_grid = slot_grid.at[place_here.reshape(-1)].set(grad_flat)
    summed = lax.psum_scatter(
        slot_grid.astype(jnp.bfloat16), "shard", scatter_dimension=0, tiled=True
    ).astype(jnp.float32)
    grad_slots = (summed * grad_scale).reshape(1, capacity, block_size, block_size)
    act_out = jnp.transpose(act_cols, (1, 0, 2)).reshape(
        replica_count, tok_rows, slice_cols * block_size
    )
    return (act_out, grad_tokens, grad_slots)


def solution(mesh):
    return jax.shard_map(
        local,
        mesh=mesh,
        in_specs=(
            P("replica", "shard", None),
            P("replica", "shard", None, None),
            P(),
            P(),
            P(),
            P(None, "shard", "replica"),
        ),
        out_specs=(
            P(None, "shard", "replica"),
            P("replica", "shard", None),
            P("replica", "shard", None, None),
        ),
        check_vma=False,
    )
```

profile of v0, /device:TPU:0, one launch (start us, length us, event | category | flops | bytes accessed | tf_op | source)
XLA Modules:
  0.0 1459.0 jit_solution(657302423886190313)
XLA Ops:
  13.4 27.5 %all-gather.4.cloned.1.call-done = bf16[4,128,3072]{2,1,0:T(8,128)(2,1)} async-done(((bf16[1,128,3072]{2,1,0:T(8,128)(2,1)}), bf16[4,128,3072]{2,1,0:T(8,128)(2,1)}) %all-gather.4.cloned.1.call-update) | async-done | bytes 3145744 | tf_op jit(solution)/shard_map/all_gather | solution.py:38
  46.1 358.8 %all-gather.6.cloned.1.call-done = bf16[1,576,128,128]{3,2,0,1:T(8,128)(2,1)} async-done(((bf16[1,72,128,128]{3,2,0,1:T(8,128)(2,1)}), bf16[1,576,128,128]{3,2,0,1:T(8,128)(2,1)}) %all-gather.6.cloned.1.call-update) | async-done | bytes 18874384 | tf_op jit(solution)/shard_map/all_gather | solution.py:35
  404.9 16.8 %gather_fusion.1 = bf16[288,128,128]{2,1,0:T(8,128)(2,1)} fusion(bf16[576,128,128]{2,1,0:T(8,128)(2,1)} %bitcast.109, s32[1024]{0:T(1024)S(1)} %pad_clamp_fusion.1), kind=kCustom, calls=%fused_computation.1 | custom fusion | bytes 18875520 | tf_op jit(solution)/shard_map/jit(_take)/gather | solution.py:36
  421.7 10.4 bitcast_select_fusion.1
  432.1 3.3 broadcast_in_dim.54
  435.4 577.5 %while.14 = (s32[]{:T(128)}, f32[512,24,128]{2,0,1:T(8,128)}, bf16[24,512,128]{2,1,0:T(8,128)(2,1)}, f32[24,1536,128]{2,1,0:T(8,128)}, s32[24,12]{1,0:T(8,128)},...) while((s32[]{:T(128)}, f32[512,24,128]{2,0,1:T(8,128)}, ...), condition=%wide.region_2.3_spmd, body=%wide.region_0.0_spmd.sunk | while | flops 608109696 | bytes 43393552 | solution.py:60
  448.4 8.1 scatter_fusion
  472.4 8.1 scatter_fusion
  496.5 8.1 scatter_fusion
  520.5 8.1 scatter_fusion
  544.5 8.1 scatter_fusion
  568.5 8.1 scatter_fusion
  576.6 3.0 fusion.34
  592.6 8.1 scatter_fusion
  616.6 8.1 scatter_fusion
  624.7 3.0 fusion.34
  640.7 8.2 scatter_fusion
  648.9 3.0 fusion.34
  664.8 8.1 scatter_fusion
  688.8 8.1 scatter_fusion
  712.9 8.1 scatter_fusion
  721.0 3.0 fusion.34
  736.9 8.2 scatter_fusion
  745.1 3.0 fusion.34
  761.1 8.1 scatter_fusion
  785.1 8.1 scatter_fusion
  793.2 3.0 fusion.34
  809.2 8.2 scatter_fusion
  833.3 8.2 scatter_fusion
  857.4 8.2 scatter_fusion
  865.6 3.0 fusion.34
  881.5 8.1 scatter_fusion
  905.6 8.1 scatter_fusion
  929.6 8.1 scatter_fusion
  937.7 3.0 fusion.34
  953.6 8.1 scatter_fusion
  961.8 3.0 fusion.34
  977.7 8.1 scatter_fusion
  985.8 3.0 fusion.34
  1001.8 8.2 scatter_fusion
  1012.9 12.6 broadcast_in_dim.61
  1025.5 52.1 %scatter_fusion.1 = f32[576,128,128]{2,1,0:T(8,128)} fusion(f32[576,128,128]{2,1,0:T(8,128)} %broadcast_in_dim.61, s32[288]{0:T(512)S(1)} %copy-done.7, f32[288,128,128]{2,1,0:T(8,128)} %bitcast.106), kind=kCustom, calls=%fused_computation.3 | custom fusion | bytes 56624256 | tf_op jit(solution)/shard_map/scatter | solution.py:71
  1077.7 20.9 %convert_element_type.26 = bf16[576,128,128]{2,1,0:T(8,128)(2,1)} convert(f32[576,128,128]{2,1,0:T(8,128)} %scatter_fusion.1) | non-fusion elementwise | flops 9437184 | bytes 56623104 | tf_op jit(solution)/shard_map/convert_element_type | solution.py:73
  1098.8 3.4 convert_element_type.24
  1107.1 3.9 copy.38
  1113.8 298.6 %reduce-scatter.5.cloned.1.call-done = bf16[72,128,128]{2,1,0:T(8,128)(2,1)} async-done(((bf16[576,128,128]{2,1,0:T(8,128)(2,1)}), bf16[72,128,128]{2,1,0:T(8,128)(2,1)}) %reduce-scatter.5.cloned.1.call-update) | async-done | bytes 2359312 | tf_op jit(solution)/shard_map/reduce_scatter | solution.py:72
  1412.4 4.5 multiply_bitcast_fusion
  1416.9 35.6 %reduce-scatter.3.cloned.1.call-done = bf16[1,128,3072]{2,1,0:T(8,128)(2,1)} async-done(((bf16[4,128,3072]{2,1,0:T(8,128)(2,1)}), bf16[1,128,3072]{2,1,0:T(8,128)(2,1)}) %reduce-scatter.3.cloned.1.call-update) | async-done | bytes 786448 | tf_op jit(solution)/shard_map/reduce_scatter | solution.py:64
  (487 shorter events, 370.7 us)
Async XLA Ops:
  7.2 2.4 copy-start.8
  7.2 2.4 copy-start.9
  7.2 2.9 copy-start.5
  7.2 33.7 %all-gather.4.cloned.1.call-start = ((), (), s32[]{:S(2)}) async-start(), calls=%async_computation.2 | async-start | bytes 3932160 | tf_op jit(solution)/shard_map/all_gather | solution.py:38
  7.9 397.0 %all-gather.6.cloned.1.call-start = ((), (), s32[]{:S(2)}) async-start(), calls=%async_computation.5 | async-start | bytes 21233664 | tf_op jit(solution)/shard_map/all_gather | solution.py:35
  8.7 1403.7 %reduce-scatter.5.cloned.1.call-start = ((), (), s32[]{:S(2)}) async-start(), calls=%async_computation.4 | async-start | bytes 21233664 | tf_op jit(solution)/shard_map/reduce_scatter | solution.py:72
  13.3 30.3 %copy-start.6 = (s32[288]{0:T(512)}, s32[288]{0:T(512)S(1)}, u32[]{:S(2)}) copy-start(s32[288]{0:T(512)S(1)} %fusion.15) | copy-start | bytes 3460
  443.2 1.7 copy-start.2
  448.4 8.1 copy-start.4
  467.2 1.7 copy-start.2
  472.4 8.1 copy-start.4
  491.2 1.7 copy-start.2
  496.4 8.1 copy-start.4
  515.3 1.7 copy-start.2
  520.5 8.1 copy-start.4
  539.3 1.7 copy-start.2
  544.5 8.1 copy-start.4
  563.3 1.7 copy-start.2
  568.5 8.1 copy-start.4
  587.4 1.7 copy-start.2
  592.6 8.1 copy-start.4
  611.4 1.7 copy-start.2
  616.6 8.1 copy-start.4
  635.5 1.7 copy-start.2
  640.7 8.2 copy-start.4
  659.6 1.7 copy-start.2
  664.8 8.1 copy-start.4
  688.8 8.1 copy-start.4
  712.9 8.1 copy-start.4
  736.9 8.2 copy-start.4
  761.1 8.1 copy-start.4
  785.1 8.2 copy-start.4
  809.2 8.2 copy-start.4
  833.3 8.2 copy-start.4
  852.2 1.7 copy-start.2
  857.4 8.2 copy-start.4
  881.5 8.1 copy-start.4
  900.3 1.7 copy-start.2
  905.6 8.1 copy-start.4
  929.5 8.1 copy-start.4
  953.6 8.2 copy-start.4
  972.5 1.7 copy-start.2
  977.7 8.1 copy-start.4
  996.6 1.7 copy-start.2
  1001.8 8.2 copy-start.4
  1012.9 12.6 copy-start.7
  1098.6 353.9 %reduce-scatter.3.cloned.1.call-start = ((), (), s32[]{:S(2)}) async-start(), calls=%async_computation.3 | async-start | bytes 3932160 | tf_op jit(solution)/shard_map/reduce_scatter | solution.py:64
  1111.0 341.5 %copy-start.1 = (s32[96,12]{0,1:T(8,128)S(1)}, s32[96,12]{0,1:T(8,128)}, u32[]{:S(2)}) copy-start(s32[96,12]{0,1:T(8,128)} %param.10) | copy-start | bytes 13828
  (35 other events, 35.9 us)
Sparse Core Ops, SparseCore 0:
  9.6 31.2 all-gather.3
  42.4 362.4 all-gather.5
  1098.7 313.6 reduce-scatter.4
  1415.4 37.0 reduce-scatter.2
where the time goes:
time: 1470 us; the launch traced here: 1460 us
  waiting for transfers between devices  722 us (49%)
  other arithmetic  308 us (21%)
  local copies, waits for them, and re-layouts  276 us (19%)
  matrix products  137 us (9%)
    all_gather x1, waiting for transfers between devices, local(): owner_slab = lax.all_gather(own_slots, 'shard', axis=0, tiled=True)  359 us
    reduce_scatter x1, waiting for transfers between devices, local(): lax.psum_scatter(slot_grid.astype(jnp.bfloat16), 'shard', scatter_dimensi...  299 us
    scatter-add x24, other arithmetic, column_step(): grad_rows.at[:, rows_col]  195 us
    gather x48, local copies, waits for them, and re-layouts, column_step(): jnp.take(token_blocks, rows_col, axis=1)  82.4 us
    dot_general x24, matrix products, column_step(): lax.dot_general(col_inputs, slope, (((0,), (0,)), ((), ())), preferred_el...  71.1 us
    scatter x1, local copies, waits for them, and re-layouts, local(): slot_grid = slot_grid.at[place_here.reshape(-1)].set(grad_flat)  52.1 us
    select_n x48, other arithmetic, column_step(): jnp.take(token_blocks, rows_col, axis=1)  40.8 us
    select_n x24, local copies, waits for them, and re-layouts, column_step(): jnp.take(token_blocks, rows_col, axis=1)  38.5 us
  transfers between devices with their start and end apart: 4, of which 4 were waited for; matrix products, arithmetic and copies ran while one was open for 2% of the time, Pallas kernels for 0%

commit v1 on v0

--- a/solution.py
+++ b/solution.py
@@ -3,6 +3,36 @@
 import jax.numpy as jnp
 from jax import lax
 from jax.sharding import PartitionSpec as P
+
+
+def trace_array_up(obj, axis_k):
+    mixed_arr = list(obj.shape[1:])
+    mixed_arr[axis_k] *= obj.shape[0]
+    r1 = jnp.moveaxis(obj, 0, axis_k).reshape(mixed_arr)
+    return r1
+
+
+def _serve_spots(join_dim, xx, named_axis):
+    n_slots = lax.psum(1, axis_name=named_axis)
+    block_last = range(n_slots)
+    oldest = map(lambda ii: (ii, (ii + 1) % n_slots), block_last)
+    seen = list(oldest)
+    cards = [(num, tick) for tick, num in seen]
+    far_arr, z = ([], [])
+    for idx in range(n_slots - 1):
+        if idx % 2 == 0:
+            far_arr.append(
+                lax.ppermute(far_arr[-1] if far_arr else xx, axis_name=named_axis, perm=seen)
+            )
+        else:
+            z.append(lax.ppermute(z[-1] if z else xx, axis_name=named_axis, perm=cards))
+    part_now = jnp.stack([*far_arr[::-1], xx, *z], axis=0)
+    z1 = lax.axis_index(named_axis)
+    all_values = len(far_arr)
+    heard = z1 - all_values
+    part_now = part_now[(jnp.arange(n_slots) - heard) % n_slots]
+    carry = trace_array_up(part_now, join_dim)
+    return carry
 
 
 def gelu_value(hidden):
@@ -32,7 +62,7 @@
     owner_here = lax.dynamic_slice_in_dim(block_owner, start_col, slice_cols, 0)
     slot_here = lax.dynamic_slice_in_dim(block_slot, start_col, slice_cols, 0)
     place_here = owner_here * capacity + slot_here
-    owner_slab = lax.all_gather(own_slots, "shard", axis=0, tiled=True)
+    owner_slab = _serve_spots(0, own_slots, "shard")
     weight_cols = jnp.take(owner_slab, place_here.reshape(-1), axis=0)
     weight_cols = weight_cols.reshape(slice_cols, keep_count * block_size, block_size)
     gathered = lax.all_gather(tokens, "replica", axis=0, tiled=True)

time: 1470 us -> 1510 us (1.027)
  waiting for transfers between devices: 722 us -> 568 us
  starting transfers between devices: 0.34 us -> 116 us
  local copies, waits for them, and re-layouts: 276 us -> 329 us
  matrix products: 137 us -> 171 us
    all_gather x1 -> x0, waiting for transfers between devices: 359 us -> none  [local(): owner_slab = lax.all_gather(own_slots, 'shard', axis=0, tiled=True)]
    ppermute x0 -> x7, waiting for transfers between devices: none -> 235 us  [the longest x4 235 us: _serve_spots(): lax.ppermute(far_arr[-1] if far_arr else xx, axis_name=named_axis, perm=s...]
    ppermute x0 -> x7, starting transfers between devices: none -> 116 us  [the longest x3 108 us: _serve_spots(): z.append(lax.ppermute(z[-1] if z else xx, axis_name=named_axis, perm=cards))]
    gather x0 -> x16, local copies, waits for them, and re-layouts: none -> 36.9 us
    dot_general x24, matrix products: 30.6 us -> 64.4 us  [column_step(): hidden = jnp.dot(col_inputs, weight_col, preferred_element_type=jnp.float32)]
    all_gather x1, waiting for transfers between devices: 27.5 us -> 0.02 us  [local(): gathered = lax.all_gather(tokens, 'replica', axis=0, tiled=True)]
    unnamed x18 -> x23, local copies, waits for them, and re-layouts: 4.34 us -> 23.7 us
  transfers between devices with their start and end apart: 4 -> 10, of which waited for: 4 -> 6; matrix products, arithmetic and copies ran while one was open for 2% -> 3% of each run, Pallas kernels for 0% -> 0%
where the time goes in v1:
time: 1510 us; the launch traced here: 1500 us
  waiting for transfers between devices  568 us (38%)
  local copies, waits for them, and re-layouts  329 us (22%)
  other arithmetic  306 us (20%)
  matrix products  171 us (11%)
  starting transfers between devices  116 us (8%)
    reduce_scatter x1, waiting for transfers between devices, local(): lax.psum_scatter(slot_grid.astype(jnp.bfloat16), 'shard', scatter_dimensi...  297 us
    ppermute x4, waiting for transfers between devices, _serve_spots(): lax.ppermute(far_arr[-1] if far_arr else xx, axis_name=named_axis, perm=s...  235 us
    scatter-add x24, other arithmetic, column_step(): grad_rows.at[:, rows_col]  192 us
    ppermute x3, starting transfers between devices, _serve_spots(): z.append(lax.ppermute(z[-1] if z else xx, axis_name=named_axis, perm=cards))  108 us
    gather x48, local copies, waits for them, and re-layouts, column_step(): jnp.take(token_blocks, rows_col, axis=1)  82.4 us
    dot_general x24, matrix products, column_step(): lax.dot_general(col_inputs, slope, (((0,), (0,)), ((), ())), preferred_el...  71.2 us
    dot_general x24, matrix products, column_step(): hidden = jnp.dot(col_inputs, weight_col, preferred_element_type=jnp.float32)  64.4 us
    scatter x1, local copies, waits for them, and re-layouts, local(): slot_grid = slot_grid.at[place_here.reshape(-1)].set(grad_flat)  52.3 us
  transfers between devices with their start and end apart: 10, of which 6 were waited for; matrix products, arithmetic and copies ran while one was open for 3% of the time, Pallas kernels for 0%

profile of v1, /device:TPU:0, one launch (start us, length us, event | category | flops | bytes accessed | tf_op | source)
XLA Modules:
  0.0 1504.9 jit_solution(11443031497835739245)
XLA Ops:
  10.2 54.5 %collective-permute-done = bf16[72,128,128]{2,1,0:T(8,128)(2,1)S(1)} collective-permute-done((bf16[72,128,128]{2,1,0:T(8,128)(2,1)}, bf16[72,128,128]{2,1,0:T(8,128)(2,1)S(1)}, u32[]{:S(2)}, u32[]{:S(2)}) %collective-permute-start) | collective-permute-done | bytes 2359328 | tf_op jit(solution)/shard_map/ppermute | solution.py:25
  64.7 4.7 collective-permute-start.4
  69.5 96.0 %collective-permute-done.1 = bf16[72,128,128]{2,1,0:T(8,128)(2,1)} collective-permute-done((bf16[72,128,128]{2,1,0:T(8,128)(2,1)S(1)}, bf16[72,128,128]{2,1,0:T(8,128)(2,1)}, u32[]{:S(2)}, u32[]{:S(2)}) %collective-permute-start.1) | collective-permute-done | bytes 2359328 | tf_op jit(solution)/shard_map/ppermute | solution.py:25
  168.1 51.5 %collective-permute-start.5 = (bf16[72,128,128]{2,1,0:T(8,128)(2,1)}, bf16[72,128,128]{2,1,0:T(8,128)(2,1)}, u32[]{:S(2)}, u32[]{:S(2)}) collective-permute-start(bf16[72,128,128]{2,1,0:T(8,128)(2,1)} %collective-permute-done.4), channel_id=1, source_target_pairs={{1,0},{2,1},{3,2},{4,3},{5,4},{6,5},{7,6},{0,7},{9,8},{10,9},{11,1... | collective-permute-start | bytes 7077896 | tf_op jit(solution)/shard_map/ppermute | solution.py:28
  219.6 48.7 %collective-permute-done.2 = bf16[72,128,128]{2,1,0:T(8,128)(2,1)} collective-permute-done((bf16[72,128,128]{2,1,0:T(8,128)(2,1)}, bf16[72,128,128]{2,1,0:T(8,128)(2,1)}, u32[]{:S(2)}, u32[]{:S(2)}) %collective-permute-start.2) | collective-permute-done | bytes 2359328 | tf_op jit(solution)/shard_map/ppermute | solution.py:25
  271.9 51.8 %collective-permute-start.6 = (bf16[72,128,128]{2,1,0:T(8,128)(2,1)}, bf16[72,128,128]{2,1,0:T(8,128)(2,1)}, u32[]{:S(2)}, u32[]{:S(2)}) collective-permute-start(bf16[72,128,128]{2,1,0:T(8,128)(2,1)} %collective-permute-done.5), channel_id=1, source_target_pairs={{1,0},{2,1},{3,2},{4,3},{5,4},{6,5},{7,6},{0,7},{9,8},{10,9},{11,1... | collective-permute-start | bytes 7077896 | tf_op jit(solution)/shard_map/ppermute | solution.py:28
  334.9 36.3 %collective-permute-done.3 = bf16[72,128,128]{2,1,0:T(8,128)(2,1)} collective-permute-done((bf16[72,128,128]{2,1,0:T(8,128)(2,1)}, bf16[72,128,128]{2,1,0:T(8,128)(2,1)}, u32[]{:S(2)}, u32[]{:S(2)}) %collective-permute-start.3) | collective-permute-done | bytes 2359328 | tf_op jit(solution)/shard_map/ppermute | solution.py:25
  384.4 6.5 copy-done.4
  390.9 36.9 %while.16 = (s32[]{:T(128)}, bf16[8,72,128,128]{3,2,1,0:T(8,128)(2,1)}, s32[8,1]{0,1:T(1,128)S(1)}, bf16[8,72,128,128]{3,2,1,0:T(8,128)(2,1)}, s32[]{:T(128)}) while((s32[]{:T(128)}, bf16[8,72,128,128]{3,2,1,0:T(8,128)(2,1)}, s32[8,1]{0,1:T(1,128)S(1)}, bf16[8,72,128,128]{3,2,1,0:T(8,128)(2,1)}, s32[]{:T(128)}) %tuple.52), condition=%wide.while_cond, body=%wide.while_body.sunk | while | flops 2 | bytes 4719189 | solution.py:33
  391.5 4.0 dynamic-slice_dynamic-update-slice_fusion.2
  400.7 4.0 dynamic-slice_dynamic-update-slice_fusion.2
  405.3 4.1 dynamic-slice_dynamic-update-slice_fusion.2
  414.5 4.1 dynamic-slice_dynamic-update-slice_fusion.2
  419.2 4.0 dynamic-slice_dynamic-update-slice_fusion.2
  423.8 4.0 dynamic-slice_dynamic-update-slice_fusion.2
  427.8 16.8 %gather_fusion.1 = bf16[288,128,128]{2,1,0:T(8,128)(2,1)} fusion(bf16[576,128,128]{2,1,0:T(8,128)(2,1)} %bitcast.126, s32[1024]{0:T(1024)S(1)} %pad_clamp_fusion.1), kind=kCustom, calls=%fused_computation.1 | custom fusion | bytes 18875520 | tf_op jit(solution)/shard_map/jit(_take)/gather | solution.py:66
  444.6 10.4 bitcast_select_fusion.1
  458.3 601.9 %while.15 = (s32[]{:T(128)}, f32[512,24,128]{2,0,1:T(8,128)}, bf16[24,512,128]{2,1,0:T(8,128)(2,1)}, f32[24,1536,128]{2,1,0:T(8,128)}, s32[24,12]{1,0:T(8,128)},...) while((s32[]{:T(128)}, f32[512,24,128]{2,0,1:T(8,128)}, ...), condition=%wide.region_2.3_spmd, body=%wide.region_0.2_spmd.sunk | while | flops 608109696 | bytes 37102068 | solution.py:90
  472.4 7.9 scatter_fusion
  497.4 8.0 scatter_fusion
  522.5 8.0 scatter_fusion
  547.5 8.0 scatter_fusion
  572.6 7.9 scatter_fusion
  597.6 8.0 scatter_fusion
  622.7 8.0 scatter_fusion
  647.7 8.0 scatter_fusion
  672.8 8.1 scatter_fusion
  697.9 8.0 scatter_fusion
  723.0 7.9 scatter_fusion
  748.0 7.9 scatter_fusion
  773.0 8.1 scatter_fusion
  798.2 8.0 scatter_fusion
  823.2 8.0 scatter_fusion
  848.3 8.1 scatter_fusion
  873.5 8.1 scatter_fusion
  898.6 8.1 scatter_fusion
  923.8 8.0 scatter_fusion
  948.9 8.0 scatter_fusion
  973.9 8.0 scatter_fusion
  999.0 8.0 scatter_fusion
  1024.1 8.0 scatter_fusion
  1049.2 8.1 scatter_fusion
  1060.2 12.6 broadcast_in_dim.62
  1072.8 52.3 %scatter_fusion.1 = f32[576,128,128]{2,1,0:T(8,128)} fusion(f32[576,128,128]{2,1,0:T(8,128)} %broadcast_in_dim.62, s32[288]{0:T(512)S(1)} %copy-done.7, f32[288,128,128]{2,1,0:T(8,128)} %bitcast.123), kind=kCustom, calls=%fused_computation.3 | custom fusion | bytes 56624256 | tf_op jit(solution)/shard_map/scatter | solution.py:101
  1125.1 20.9 %convert_element_type.26 = bf16[576,128,128]{2,1,0:T(8,128)(2,1)} convert(f32[576,128,128]{2,1,0:T(8,128)} %scatter_fusion.1) | non-fusion elementwise | flops 9437184 | bytes 56623104 | tf_op jit(solution)/shard_map/convert_element_type | solution.py:103
  1161.3 296.8 %reduce-scatter.5.cloned.1.call-done = bf16[72,128,128]{2,1,0:T(8,128)(2,1)} async-done(((bf16[576,128,128]{2,1,0:T(8,128)(2,1)}), bf16[72,128,128]{2,1,0:T(8,128)(2,1)}) %reduce-scatter.5.cloned.1.call-update) | async-done | bytes 2359312 | tf_op jit(solution)/shard_map/reduce_scatter | solution.py:102
  1458.2 4.5 multiply_bitcast_fusion
  1462.6 35.7 %reduce-scatter.3.cloned.1.call-done = bf16[1,128,3072]{2,1,0:T(8,128)(2,1)} async-done(((bf16[4,128,3072]{2,1,0:T(8,128)(2,1)}), bf16[1,128,3072]{2,1,0:T(8,128)(2,1)}) %reduce-scatter.3.cloned.1.call-update) | async-done | bytes 786448 | tf_op jit(solution)/shard_map/reduce_scatter | solution.py:94
  (475 shorter events, 473.4 us)
Async XLA Ops:
  7.2 264.6 %copy-start = (s32[96,12]{0,1:T(8,128)S(1)}, s32[96,12]{0,1:T(8,128)}, u32[]{:S(2)}) copy-start(s32[96,12]{0,1:T(8,128)} %param.10) | copy-start | bytes 13828
  7.2 322.6 %all-gather.2.cloned.1.call-start = ((), (), s32[]{:S(2)}) async-start(), calls=%async_computation.2 | async-start | bytes 3932160 | tf_op jit(solution)/shard_map/all_gather | solution.py:68
  7.2 57.5 %collective-permute-start = (bf16[72,128,128]{2,1,0:T(8,128)(2,1)}, bf16[72,128,128]{2,1,0:T(8,128)(2,1)S(1)}, u32[]{:S(2)}, u32[]{:S(2)}) collective-permute-start(bf16[72,128,128]{2,1,0:T(8,128)(2,1)} %bitcast.130), channel_id=1, source_target_pairs={{0,1},{1,2},{2,3},{3,4},{4,5},{5,6},{6,7},{7,0},{8,9},{9,10},{10,1... | collective-permute-start | bytes 7077896 | tf_op jit(solution)/shard_map/ppermute | solution.py:25
  64.7 100.8 %collective-permute-start.1 = (bf16[72,128,128]{2,1,0:T(8,128)(2,1)S(1)}, bf16[72,128,128]{2,1,0:T(8,128)(2,1)}, u32[]{:S(2)}, u32[]{:S(2)}) collective-permute-start(bf16[72,128,128]{2,1,0:T(8,128)(2,1)S(1)} %collective-permute-done), channel_id=1, source_target_pairs={{0,1},{1,2},{2,3},{3,4},{4,5},{5,6},{6,7},{7,0},{8,9},{9,10},{10,1... | collective-permute-start | bytes 7077896 | tf_op jit(solution)/shard_map/ppermute | solution.py:25
  64.7 103.4 %collective-permute-start.4 = (bf16[72,128,128]{2,1,0:T(8,128)(2,1)}, bf16[72,128,128]{2,1,0:T(8,128)(2,1)}, u32[]{:S(2)}, u32[]{:S(2)}) collective-permute-start(bf16[72,128,128]{2,1,0:T(8,128)(2,1)} %bitcast.131), channel_id=1, source_target_pairs={{1,0},{2,1},{3,2},{4,3},{5,4},{6,5},{7,6},{0,7},{9,8},{10,9},{11,1... | collective-permute-start | bytes 7077896 | tf_op jit(solution)/shard_map/ppermute | solution.py:28
  69.5 1388.7 %reduce-scatter.5.cloned.1.call-start = ((), (), s32[]{:S(2)}) async-start(), calls=%async_computation.4 | async-start | bytes 21233664 | tf_op jit(solution)/shard_map/reduce_scatter | solution.py:102
  165.5 102.8 %collective-permute-start.2 = (bf16[72,128,128]{2,1,0:T(8,128)(2,1)}, bf16[72,128,128]{2,1,0:T(8,128)(2,1)}, u32[]{:S(2)}, u32[]{:S(2)}) collective-permute-start(bf16[72,128,128]{2,1,0:T(8,128)(2,1)} %collective-permute-done.1), channel_id=1, source_target_pairs={{0,1},{1,2},{2,3},{3,4},{4,5},{5,6},{6,7},{7,0},{8,9},{9,10},{10,1... | collective-permute-start | bytes 7077896 | tf_op jit(solution)/shard_map/ppermute | solution.py:25
  168.1 103.8 %collective-permute-start.5 = (bf16[72,128,128]{2,1,0:T(8,128)(2,1)}, bf16[72,128,128]{2,1,0:T(8,128)(2,1)}, u32[]{:S(2)}, u32[]{:S(2)}) collective-permute-start(bf16[72,128,128]{2,1,0:T(8,128)(2,1)} %collective-permute-done.4), channel_id=1, source_target_pairs={{1,0},{2,1},{3,2},{4,3},{5,4},{6,5},{7,6},{0,7},{9,8},{10,9},{11,1... | collective-permute-start | bytes 7077896 | tf_op jit(solution)/shard_map/ppermute | solution.py:28
  268.3 102.9 %collective-permute-start.3 = (bf16[72,128,128]{2,1,0:T(8,128)(2,1)}, bf16[72,128,128]{2,1,0:T(8,128)(2,1)}, u32[]{:S(2)}, u32[]{:S(2)}) collective-permute-start(bf16[72,128,128]{2,1,0:T(8,128)(2,1)} %collective-permute-done.2), channel_id=1, source_target_pairs={{0,1},{1,2},{2,3},{3,4},{4,5},{5,6},{6,7},{7,0},{8,9},{9,10},{10,1... | collective-permute-start | bytes 7077896 | tf_op jit(solution)/shard_map/ppermute | solution.py:25
  271.9 57.9 %copy-start.6 = (s32[288]{0:T(512)}, s32[288]{0:T(512)S(1)}, u32[]{:S(2)}) copy-start(s32[288]{0:T(512)S(1)} %fusion.15) | copy-start | bytes 3460
  271.9 110.4 %collective-permute-start.6 = (bf16[72,128,128]{2,1,0:T(8,128)(2,1)}, bf16[72,128,128]{2,1,0:T(8,128)(2,1)}, u32[]{:S(2)}, u32[]{:S(2)}) collective-permute-start(bf16[72,128,128]{2,1,0:T(8,128)(2,1)} %collective-permute-done.5), channel_id=1, source_target_pairs={{1,0},{2,1},{3,2},{4,3},{5,4},{6,5},{7,6},{0,7},{9,8},{10,9},{11,1... | collective-permute-start | bytes 7077896 | tf_op jit(solution)/shard_map/ppermute | solution.py:28
  375.2 2.6 copy-start.5
  384.4 6.5 copy-start.4
  470.2 0.7 copy-start.2
  472.4 8.0 copy-start.3
  497.3 8.0 copy-start.3
  522.4 8.0 copy-start.3
  547.5 8.0 copy-start.3
  572.5 8.0 copy-start.3
  597.6 8.0 copy-start.3
  622.6 8.0 copy-start.3
  647.7 8.0 copy-start.3
  670.6 0.7 copy-start.2
  672.8 8.1 copy-start.3
  695.7 0.7 copy-start.2
  697.9 8.0 copy-start.3
  720.8 0.7 copy-start.2
  723.0 8.0 copy-start.3
  748.0 8.0 copy-start.3
  773.0 8.1 copy-start.3
  796.0 0.7 copy-start.2
  798.2 8.0 copy-start.3
  823.2 8.0 copy-start.3
  848.3 8.1 copy-start.3
  873.4 8.1 copy-start.3
  898.6 8.1 copy-start.3
  921.6 0.7 copy-start.2
  923.8 8.0 copy-start.3
  946.7 0.7 copy-start.2
  948.9 8.0 copy-start.3
  973.9 8.0 copy-start.3
  999.0 8.0 copy-start.3
  1021.9 0.7 copy-start.2
  1024.1 8.0 copy-start.3
  1049.1 8.1 copy-start.3
  1060.2 12.6 copy-start.7
  1146.0 352.4 %reduce-scatter.3.cloned.1.call-start = ((), (), s32[]{:S(2)}) async-start(), calls=%async_computation.3 | async-start | bytes 3932160 | tf_op jit(solution)/shard_map/reduce_scatter | solution.py:94
  1158.5 339.9 %copy-start.1 = (s32[96,12]{0,1:T(8,128)S(1)}, s32[96,12]{0,1:T(8,128)}, u32[]{:S(2)}) copy-start(s32[96,12]{0,1:T(8,128)} %param.10) | copy-start | bytes 13828
  (16 other events, 11.2 us)
Sparse Core Ops, SparseCore 0:
  69.6 25.8 all-gather.1
  1146.2 311.9 reduce-scatter.4
  1461.3 37.0 reduce-scatter.2
